TPU v7x, 256 devices: a whole 4x4x8 slice. The times are simulated.
256 devices in a mesh: tp: 2 (over z_lo), sp: 32 (over x, y, core), dp: 4 (over z_hi).
Axes of the slice: x: 4, y: 4, z: 8 (z_hi: 4, z_lo: 2; z = z_hi * 2 + z_lo), core: 2. Of those that a mesh axis runs over, the one named last changes fastest.
Arguments:
- queries: bfloat16 [16384, 4096], P(('dp', 'sp'), 'tp'), parts along dimension 0, may hold values from -256 to 256
- key_projection_rows: bfloat16 [16384, 512], P(('dp', 'sp'), 'tp'), parts along dimension 0, may hold values from -8 to 8
- values: bfloat16 [16384, 512], P(('dp', 'sp'), 'tp'), parts along dimension 0, may hold values from -6 to 6
- segment_ids: int32 [16384], P('dp'), parts along dimension 0, may hold values from 0 to 11, never falling along the last dimension, each value on 1 to 1024 neighbouring positions
- residual: bfloat16 [16384, 8192], P(('dp', 'tp'), 'sp'), parts along dimension 0, may hold values from -40 to 40
- out_weight: bfloat16 [4096, 8192], P('tp', 'sp'), may hold values from -0.09375 to 0.09375
- norm_gain: float32 [8192], P('sp'), may hold values from 0.1 to 1.9
- scale_exponent: int32 [8192], P('sp'), may hold values from 7 to 8
Outputs:
- hidden_out: bfloat16 [16384, 8192], P(('dp', 'tp'), 'sp'), parts along dimension 0
- quantized: bfloat16 [16384, 8192], P(('dp', 'tp'), 'sp'), parts along dimension 0
There are 4 independent parts, one for each index of `dp`. A program takes and returns all parts, laid end to end along the dimension named above; an argument that names none is the same for every part. Nothing has to cross between parts.
Inputs may be any that keep to these rules, and one draw needn't show every extreme that they name: `segment_ids`: never falls along the window; every document holds at most a quarter of the window's tokens, and one holds exactly that many.
All inputs are finite; a program needn't handle non-finite values.
Results may differ from a plain program's by a relative error of at most 0.0065.
Values may be sent and summed in bfloat16 or wider, within the bound.
No kernel may reach another device: no remote copies, remote signals or barrier semaphores. Data moves between devices by JAX's collectives and lax.ppermute only.
A program may use at most 64 MiB of HBM per device.

v0:
```python
import jax
import jax.numpy as jnp
from jax import lax
from jax.sharding import PartitionSpec as P

D = 8192
QUERY_HEAD_COUNT = 32
KEY_VALUE_HEADS = 4
HEAD_DIMENSION = 128
epsilon = 1e-05
limit_value = 448.0


def attend_item(query_block, key_block, value_block, query_pos, query_seg, segment_ids, key_pos):
    query_count = query_block.shape[0]
    block_rows = min(512, query_count)
    blocks = query_count // block_rows

    def one_block(packed):
        block_query, block_pos, block_seg = packed
        scores = lax.dot_general(
            block_query, key_block, (((1,), (1,)), ((), ())), preferred_element_type=jnp.float32
        ) * HEAD_DIMENSION ** (-0.5)
        visible = (key_pos[None, :] <= block_pos[:, None]) & (
            segment_ids[None, :] == block_seg[:, None]
        )
        scores = jnp.where(visible, scores, -1e30)
        largest = jnp.max(scores, axis=1, keepdims=True)
        weights = jnp.exp(scores - largest)
        row_total = jnp.sum(weights, axis=1, keepdims=True)
        probabilities = (weights / row_total).astype(jnp.bfloat16)
        return jnp.dot(probabilities, value_block, preferred_element_type=jnp.float32).astype(
            jnp.bfloat16
        )

    results = lax.map(
        one_block,
        (
            query_block.reshape(blocks, block_rows, HEAD_DIMENSION),
            query_pos.reshape(blocks, block_rows),
            query_seg.reshape(blocks, block_rows),
        ),
    )
    return results.reshape(query_count, HEAD_DIMENSION)


def body(
    queries,
    key_projection_rows,
    values,
    segment_ids,
    residual,
    out_weight,
    norm_gain,
    scale_exponent,
):
    sp_count = lax.axis_size("sp")
    token_rows = queries.shape[0]
    half_rows = token_rows // 2
    local_heads = queries.shape[1] // HEAD_DIMENSION
    item_count = 2 * local_heads
    per_device = item_count // sp_count
    window_token_rows = token_rows * sp_count
    query_count = window_token_rows // 2
    group_width = QUERY_HEAD_COUNT // KEY_VALUE_HEADS
    own_index = lax.axis_index("sp")
    query_items = jnp.transpose(
        queries.reshape(2, half_rows, local_heads, HEAD_DIMENSION), (0, 2, 1, 3)
    ).reshape(item_count, half_rows, HEAD_DIMENSION)
    query_recv = lax.all_to_all(query_items, "sp", split_axis=0, concat_axis=1, tiled=True)
    key_all, value_all = (
        lax.all_gather(key_projection_rows, "sp", axis=0, tiled=True),
        lax.all_gather(values, "sp", axis=0, tiled=True),
    )
    key_pos = jnp.arange(window_token_rows, dtype=jnp.int32)
    row_number = jnp.arange(query_count, dtype=jnp.int32)
    source_device = row_number // half_rows
    within = row_number % half_rows
    segment_grid = segment_ids.reshape(sp_count, 2, half_rows)
    number = 0
    item_index = own_index * per_device + number
    which_half = item_index // local_heads
    query_pos = source_device * token_rows + which_half * half_rows + within
    query_seg = lax.dynamic_index_in_dim(segment_grid, which_half, 1, keepdims=False).reshape(
        query_count
    )
    shared_rows = item_index % local_heads // group_width
    key_block = lax.dynamic_slice_in_dim(key_all, shared_rows * HEAD_DIMENSION, HEAD_DIMENSION, 1)
    value_block = lax.dynamic_slice_in_dim(
        value_all, shared_rows * HEAD_DIMENSION, HEAD_DIMENSION, 1
    )
    outputs = [
        attend_item(
            query_recv[number], key_block, value_block, query_pos, query_seg, segment_ids, key_pos
        )
    ]
    own_outputs = jnp.stack(outputs)
    column_count = out_weight.shape[1]
    start_sum = jnp.zeros((sp_count, 2, half_rows, column_count), jnp.float32)
    pieces = lax.all_gather(own_outputs, "sp", axis=0, tiled=True)

    def add_one(number, current):
        head_number = number % local_heads
        which_half = number // local_heads
        head_weight = lax.dynamic_slice_in_dim(
            out_weight, head_number * HEAD_DIMENSION, HEAD_DIMENSION, 0
        )
        chosen = lax.dynamic_index_in_dim(pieces, number, 0, keepdims=False)
        product_term = jnp.dot(chosen, head_weight, preferred_element_type=jnp.float32).reshape(
            sp_count, 1, half_rows, column_count
        )
        corner = (0, which_half, 0, 0)
        earlier = lax.dynamic_slice(current, corner, (sp_count, 1, half_rows, column_count))
        return lax.dynamic_update_slice(current, earlier + product_term, corner)

    combined = lax.fori_loop(0, pieces.shape[0], add_one, start_sum)
    flattened = combined.reshape(window_token_rows, column_count)
    share_rows = window_token_rows // lax.axis_size("tp")
    whole_sum = lax.psum(flattened, "tp")
    summed = lax.dynamic_slice_in_dim(whole_sum, lax.axis_index("tp") * share_rows, share_rows, 0)
    projected = summed.astype(jnp.bfloat16)
    hidden_out = (residual.astype(jnp.float32) + projected.astype(jnp.float32)).astype(jnp.bfloat16)
    widened = hidden_out.astype(jnp.float32)
    square_sum = lax.psum(jnp.sum(widened * widened, axis=1), "sp")
    mean_square = (square_sum / D)[:, None]
    normed = widened * lax.rsqrt(mean_square + epsilon) * norm_gain[None, :]
    clip_bound = (limit_value * jnp.exp2(-scale_exponent.astype(jnp.float32)))[None, :]
    quantized = jnp.clip(normed, -clip_bound, clip_bound).astype(jnp.bfloat16)
    return (hidden_out, quantized)


def solution(mesh):
    in_specs = (
        P(("dp", "sp"), "tp"),
        P(("dp", "sp"), "tp"),
        P(("dp", "sp"), "tp"),
        P("dp"),
        P(("dp", "tp"), "sp"),
        P("tp", "sp"),
        P("sp"),
        P("sp"),
    )
    out_specs = (P(("dp", "tp"), "sp"), P(("dp", "tp"), "sp"))
    return jax.shard_map(body, mesh=mesh, in_specs=in_specs, out_specs=out_specs, check_vma=False)
```

profile of v0, /device:TPU:1, one launch (start us, length us, event | category | flops | bytes accessed | tf_op | source)
XLA Modules:
  0.0 569.2 jit_solution(7606608849317972235)
XLA Ops:
  10.8 8.6 %all-to-all-start = ((bf16[32,64,128]{2,1,0:T(8,128)(2,1)}), bf16[32,64,128]{2,1,0:T(8,128)(2,1)S(1)}, u32[]{:S(2)}, u32[]{:S(2)}) async-start(bf16[32,64,128]{2,1,0:T(8,128)(2,1)} %bitcast.4), calls=%async_computation | async-start | bytes 1048576 | tf_op jit(solution)/shard_map/all_to_all | solution.py:70
  19.8 43.6 %all-gather.6.cloned.1.call-done = bf16[4096,256]{1,0:T(8,128)(2,1)} async-done(((bf16[128,256]{1,0:T(8,128)(2,1)}), bf16[4096,256]{1,0:T(8,128)(2,1)}) %all-gather.6.cloned.1.call-update) | async-done | bytes 2097168 | tf_op jit(solution)/shard_map/all_gather | solution.py:73
  64.6 49.3 %all-gather.4.cloned.1.call-done = bf16[4096,256]{1,0:T(8,128)(2,1)} async-done(((bf16[128,256]{1,0:T(8,128)(2,1)}), bf16[4096,256]{1,0:T(8,128)(2,1)}) %all-gather.4.cloned.1.call-update) | async-done | bytes 2097168 | tf_op jit(solution)/shard_map/all_gather | solution.py:72
  115.2 24.3 %while.27 = (s32[]{:T(128)}, bf16[4,512,128]{2,1,0:T(8,128)(2,1)S(1)}, s32[4,512]{1,0:T(4,128)S(1)}, s32[4096]{0:T(1024)S(1)}, s32[4,512]{1,0:T(4,128)S(1)}, /*i...) while((s32[]{:T(128)}, ...), condition=%wide.region_3.4_spmd.clone, body=%wide.region_0.3_spmd.clone.sunk | while | flops 1096875008 | bytes 27564136 | solution.py:36
  140.3 77.1 %all-gather.8.cloned.1.call-done = bf16[32,2048,128]{2,1,0:T(8,128)(2,1)} async-done(((bf16[1,2048,128]{2,1,0:T(8,128)(2,1)}), bf16[32,2048,128]{2,1,0:T(8,128)(2,1)}) %all-gather.8.cloned.1.call-update) | async-done | bytes 16777232 | tf_op jit(solution)/shard_map/all_gather | solution.py:100
  219.9 174.8 %while.26 = (s32[]{:T(128)}, f32[32,2,64,256]{3,2,1,0:T(8,128)}, bf16[32,2048,128]{2,1,0:T(8,128)(2,1)}, bf16[2048,256]{1,0:T(8,128)(2,1)}, s32[]{:T(128)}, /*in...) while((s32[]{:T(128)}, f32[32,2,64,256]{3,2,1,0:T(8,128)}, ...), condition=%wide.region_5.6_spmd, body=%wide.region_4.5_spmd.sunk | while | flops 134742032 | bytes 10027344 | solution.py:116
  222.7 2.6 bitcast_dynamic-update-slice_fusion.2
  233.6 2.6 bitcast_dynamic-update-slice_fusion.2
  244.4 2.6 bitcast_dynamic-update-slice_fusion.2
  255.3 2.6 bitcast_dynamic-update-slice_fusion.2
  260.7 2.6 bitcast_dynamic-update-slice_fusion.2
  282.4 2.6 bitcast_dynamic-update-slice_fusion.2
  287.9 2.6 bitcast_dynamic-update-slice_fusion.2
  298.7 2.6 bitcast_dynamic-update-slice_fusion.2
  309.6 2.6 bitcast_dynamic-update-slice_fusion.2
  315.1 2.6 bitcast_dynamic-update-slice_fusion.2
  320.6 2.6 bitcast_dynamic-update-slice_fusion.2
  326.0 2.6 bitcast_dynamic-update-slice_fusion.2
  331.5 2.6 bitcast_dynamic-update-slice_fusion.2
  337.0 2.6 bitcast_dynamic-update-slice_fusion.2
  342.5 2.6 bitcast_dynamic-update-slice_fusion.2
  348.0 2.6 bitcast_dynamic-update-slice_fusion.2
  353.5 2.6 bitcast_dynamic-update-slice_fusion.2
  359.0 2.6 bitcast_dynamic-update-slice_fusion.2
  364.5 2.6 bitcast_dynamic-update-slice_fusion.2
  370.0 2.6 bitcast_dynamic-update-slice_fusion.2
  375.5 2.6 bitcast_dynamic-update-slice_fusion.2
  381.0 2.6 bitcast_dynamic-update-slice_fusion.2
  386.5 2.6 bitcast_dynamic-update-slice_fusion.2
  392.0 2.6 bitcast_dynamic-update-slice_fusion.2
  394.7 100.2 %all-reduce.1 = bf16[4096,256]{1,0:T(8,128)(2,1)S(1)} all-reduce(f32[4096,256]{1,0:T(8,128)} %bitcast.61), channel_id=1, replica_groups=mesh['tp'=2,'sp'=32,'dp'=4] {'tp'}, use_global_device_ids=true, to_apply=%region_6.7 | all-reduce | flops 1048576 | bytes 6291456 | tf_op jit(solution)/shard_map/psum | solution.py:119
  496.6 64.7 %psum.15 = f32[2048]{0:T(1024)S(1)} all-reduce(f32[2048]{0:T(1024)S(1)} %get-tuple-element.206), channel_id=1, replica_groups=mesh['tp'=2,'sp'=32,'dp'=4] {'sp'}, use_global_device_ids=true, to_apply=%region_8.9 | all-reduce | flops 2048 | bytes 16384 | tf_op jit(solution)/shard_map/psum | solution.py:124
  (120 shorter events, 148.3 us)
Async XLA Ops:
  7.2 12.3 %copy-start.2 = (s32[4096]{0:T(1024)S(1)}, s32[4096]{0:T(1024)}, u32[]{:S(2)}) copy-start(s32[4096]{0:T(1024)} %param.15) | copy-start | bytes 49156
  7.2 56.2 %all-gather.6.cloned.1.call-start = ((), (), s32[]{:S(2)}) async-start(), calls=%async_computation.2 | async-start | bytes 2162688 | tf_op jit(solution)/shard_map/all_gather | solution.py:73
  7.9 106.0 %all-gather.4.cloned.1.call-start = ((), (), s32[]{:S(2)}) async-start(), calls=%async_computation.1 | async-start | bytes 2162688 | tf_op jit(solution)/shard_map/all_gather | solution.py:72
  10.8 104.4 %all-to-all-start = ((bf16[32,64,128]{2,1,0:T(8,128)(2,1)}), bf16[32,64,128]{2,1,0:T(8,128)(2,1)S(1)}, u32[]{:S(2)}, u32[]{:S(2)}) async-start(bf16[32,64,128]{2,1,0:T(8,128)(2,1)} %bitcast.4), calls=%async_computation | async-start | bytes 1048576 | tf_op jit(solution)/shard_map/all_to_all | solution.py:70
  19.4 198.0 %all-gather.8.cloned.1.call-start = ((), (), s32[]{:S(2)}) async-start(), calls=%async_computation.3 | async-start | bytes 17301504 | tf_op jit(solution)/shard_map/all_gather | solution.py:100
  115.2 25.1 %copy-start.4 = (s32[256]{0:T(256)S(1)}, s32[256]{0:T(256)}, u32[]{:S(2)}) copy-start(s32[256]{0:T(256)} %param.19) | copy-start | bytes 3076
  139.5 0.8 copy-start.1
  394.7 166.6 %copy-start.3 = (f32[256]{0:T(256)S(1)}, f32[256]{0:T(256)}, u32[]{:S(2)}) copy-start(f32[256]{0:T(256)} %param.18) | copy-start | bytes 3076
  496.5 66.2 %copy-start = (bf16[2048,256]{1,0:T(8,128)(2,1)}, bf16[2048,256]{1,0:T(8,128)(2,1)S(1)}, u32[]{:S(2)}) copy-start(bf16[2048,256]{1,0:T(8,128)(2,1)S(1)} %get-tuple-element.207) | copy-start | bytes 3145732
Sparse Core Ops, SparseCore 0:
  10.5 52.7 all-gather.5
  65.9 47.9 all-gather.3
  140.4 76.9 all-gather.7
where the time goes:
time: 574 us; the launch traced here: 569 us
  waiting for transfers between devices  171 us (30%)
  blocking collectives  165 us (29%)
  matrix products  103 us (18%)
  local copies, waits for them, and re-layouts  98.9 us (17%)
  between operations  14 us (2%)
  starting transfers between devices  8.69 us (2%)
  other arithmetic  8.28 us (1%)
    psum x1, blocking collectives, body(): whole_sum = lax.psum(flattened, 'tp')  100 us
    dot_general x32, matrix products, add_one(): jnp.dot(chosen, head_weight, preferred_element_type=jnp.float32)  83.6 us
    all_gather x1, waiting for transfers between devices, body(): pieces = lax.all_gather(own_outputs, 'sp', axis=0, tiled=True)  77.1 us
    psum x1, blocking collectives, body(): square_sum = lax.psum(jnp.sum(widened * widened, axis=1), 'sp')  64.7 us
    dynamic_slice x32, local copies, waits for them, and re-layouts, add_one(): lax.dynamic_slice(current, corner, (sp_count, 1, half_rows, column_count))  56.2 us
    all_gather x1, waiting for transfers between devices, body(): lax.all_gather(key_projection_rows, 'sp', axis=0, tiled=True)  49.3 us
    all_gather x1, waiting for transfers between devices, body(): lax.all_gather(values, 'sp', axis=0, tiled=True)  43.6 us
    dynamic_slice x32, local copies, waits for them, and re-layouts, add_one(): chosen = lax.dynamic_index_in_dim(pieces, number, 0, keepdims=False)  34.6 us
  transfers between devices with their start and end apart: 4, of which 3 were waited for; matrix products, arithmetic and copies ran while one was open for 1% of the time, Pallas kernels for 0%

commit v1 on v0

--- a/solution.py
+++ b/solution.py
@@ -9,6 +9,15 @@
 HEAD_DIMENSION = 128
 epsilon = 1e-05
 limit_value = 448.0
+
+
+def get_the_figure(vals):
+    num = lax.axis_size("sp")
+    extra = range(vals.ndim)
+    item_now = map(lambda dev: num if dev == 0 else 1, extra)
+    high = list(item_now)
+    value_now = jnp.tile(vals, high)
+    return lax.all_to_all(value_now, "sp", split_axis=0, concat_axis=0, tiled=True)
 
 
 def attend_item(query_block, key_block, value_block, query_pos, query_seg, segment_ids, key_pos):
@@ -70,7 +79,7 @@
     query_recv = lax.all_to_all(query_items, "sp", split_axis=0, concat_axis=1, tiled=True)
     key_all, value_all = (
         lax.all_gather(key_projection_rows, "sp", axis=0, tiled=True),
-        lax.all_gather(values, "sp", axis=0, tiled=True),
+        get_the_figure(values),
     )
     key_pos = jnp.arange(window_token_rows, dtype=jnp.int32)
     row_number = jnp.arange(query_count, dtype=jnp.int32)

time: 574 us -> 542 us (0.944)
  waiting for transfers between devices: 171 us -> 127 us
  matrix products: 103 us -> 110 us
    all_gather x1 -> x0, waiting for transfers between devices: 43.6 us -> none  [body(): lax.all_gather(values, 'sp', axis=0, tiled=True)]
    all_gather x1, waiting for transfers between devices: 49.3 us -> 20 us  [body(): lax.all_gather(key_projection_rows, 'sp', axis=0, tiled=True)]
    all_to_all x0 -> x1, waiting for transfers between devices: none -> 27.8 us  [get_the_figure(): lax.all_to_all(value_now, 'sp', split_axis=0, concat_axis=0, tiled=True)]
    all_to_all x0 -> x1, starting transfers between devices: none -> 8.58 us  [get_the_figure(): lax.all_to_all(value_now, 'sp', split_axis=0, concat_axis=0, tiled=True)]
where the time goes in v1:
time: 542 us; the launch traced here: 537 us
  blocking collectives  165 us (30%)
  waiting for transfers between devices  127 us (23%)
  matrix products  110 us (20%)
  local copies, waits for them, and re-layouts  98.3 us (18%)
  between operations  14.3 us (3%)
  starting transfers between devices  13.7 us (3%)
  other arithmetic  8.25 us (2%)
    psum x1, blocking collectives, body(): whole_sum = lax.psum(flattened, 'tp')  100 us
    dot_general x32, matrix products, add_one(): jnp.dot(chosen, head_weight, preferred_element_type=jnp.float32)  84.7 us
    all_gather x1, waiting for transfers between devices, body(): pieces = lax.all_gather(own_outputs, 'sp', axis=0, tiled=True)  78.5 us
    psum x1, blocking collectives, body(): square_sum = lax.psum(jnp.sum(widened * widened, axis=1), 'sp')  64.7 us
    dynamic_slice x32, local copies, waits for them, and re-layouts, add_one(): lax.dynamic_slice(current, corner, (sp_count, 1, half_rows, column_count))  56.2 us
    dynamic_slice x32, local copies, waits for them, and re-layouts, add_one(): chosen = lax.dynamic_index_in_dim(pieces, number, 0, keepdims=False)  34.6 us
    all_to_all x1, waiting for transfers between devices, get_the_figure(): lax.all_to_all(value_now, 'sp', split_axis=0, concat_axis=0, tiled=True)  27.8 us
    all_gather x1, waiting for transfers between devices, body(): lax.all_gather(key_projection_rows, 'sp', axis=0, tiled=True)  20 us
  transfers between devices with their start and end apart: 4, of which 3 were waited for; matrix products, arithmetic and copies ran while one was open for 1% of the time, Pallas kernels for 0%

profile of v1, /device:TPU:1, one launch (start us, length us, event | category | flops | bytes accessed | tf_op | source)
XLA Modules:
  0.0 537.4 jit_solution(11160819682007191023)
XLA Ops:
  10.3 8.6 %all-to-all-start.1 = ((bf16[32,128,256]{2,1,0:T(8,128)(2,1)}), bf16[32,128,256]{2,1,0:T(8,128)(2,1)S(1)}, u32[]{:S(2)}, u32[]{:S(2)}) async-start(bf16[32,128,256]{2,1,0:T(8,128)(2,1)} %tile.2), calls=%async_computation.1 | async-start | bytes 4194304 | tf_op jit(solution)/shard_map/all_to_all | solution.py:20
  20.3 27.8 %all-to-all-done.1 = bf16[32,128,256]{2,1,0:T(8,128)(2,1)S(1)} async-done(((bf16[32,128,256]{2,1,0:T(8,128)(2,1)}), bf16[32,128,256]{2,1,0:T(8,128)(2,1)S(1)}, u32[]{:S(2)}, u32[]{:S(2)}) %all-to-all-start.1) | async-done | bytes 2097184 | tf_op jit(solution)/shard_map/all_to_all | solution.py:20
  48.2 5.0 all-to-all-start
  53.3 20.0 %all-gather.3.cloned.1.call-done = bf16[4096,256]{1,0:T(8,128)(2,1)} async-done(((bf16[128,256]{1,0:T(8,128)(2,1)}), bf16[4096,256]{1,0:T(8,128)(2,1)}) %all-gather.3.cloned.1.call-update) | async-done | bytes 2097168 | tf_op jit(solution)/shard_map/all_gather | solution.py:81
  74.7 31.0 %while.27 = (s32[]{:T(128)}, bf16[4,512,128]{2,1,0:T(8,128)(2,1)}, s32[4,512]{1,0:T(4,128)S(1)}, s32[4096]{0:T(1024)S(1)}, s32[4,512]{1,0:T(4,128)S(1)}, /*index...) while((s32[]{:T(128)}, bf16[4,512,128]{2,1,0:T(8,128)(2,1)}, ...), condition=%wide.region_3.4_spmd.clone, body=%wide.region_0.3_spmd.clone.sunk | while | flops 1096875008 | bytes 27565152 | solution.py:45
  74.7 3.6 fusion.40
  79.6 2.8 fusion.42
  82.4 3.6 fusion.40
  87.3 2.8 fusion.42
  90.2 3.6 fusion.40
  95.1 2.8 fusion.42
  97.9 3.6 fusion.40
  102.8 2.8 fusion.42
  105.7 78.5 %all-gather.5.cloned.1.call-done = bf16[32,2048,128]{2,1,0:T(8,128)(2,1)} async-done(((bf16[1,2048,128]{2,1,0:T(8,128)(2,1)}), bf16[32,2048,128]{2,1,0:T(8,128)(2,1)}) %all-gather.5.cloned.1.call-update) | async-done | bytes 16777232 | tf_op jit(solution)/shard_map/all_gather | solution.py:109
  186.6 175.9 %while.26 = (s32[]{:T(128)}, f32[32,2,64,256]{3,2,1,0:T(8,128)}, bf16[32,2048,128]{2,1,0:T(8,128)(2,1)}, bf16[2048,256]{1,0:T(8,128)(2,1)}, s32[]{:T(128)}, /*in...) while((s32[]{:T(128)}, f32[32,2,64,256]{3,2,1,0:T(8,128)}, ...), condition=%wide.region_5.6_spmd, body=%wide.region_4.5_spmd.sunk | while | flops 134742032 | bytes 10027344 | solution.py:125
  195.0 2.6 bitcast_dynamic-update-slice_fusion.2
  277.4 2.6 bitcast_dynamic-update-slice_fusion.2
  293.9 2.6 bitcast_dynamic-update-slice_fusion.2
  299.4 2.6 bitcast_dynamic-update-slice_fusion.2
  304.9 2.6 bitcast_dynamic-update-slice_fusion.2
  310.4 2.6 bitcast_dynamic-update-slice_fusion.2
  315.9 2.6 bitcast_dynamic-update-slice_fusion.2
  321.4 2.6 bitcast_dynamic-update-slice_fusion.2
  326.9 2.6 bitcast_dynamic-update-slice_fusion.2
  332.4 2.6 bitcast_dynamic-update-slice_fusion.2
  337.9 2.6 bitcast_dynamic-update-slice_fusion.2
  343.4 2.6 bitcast_dynamic-update-slice_fusion.2
  348.9 2.6 bitcast_dynamic-update-slice_fusion.2
  354.4 2.6 bitcast_dynamic-update-slice_fusion.2
  359.9 2.6 bitcast_dynamic-update-slice_fusion.2
  362.5 100.2 %all-reduce.1 = bf16[4096,256]{1,0:T(8,128)(2,1)S(1)} all-reduce(f32[4096,256]{1,0:T(8,128)} %bitcast.62), channel_id=1, replica_groups=mesh['tp'=2,'sp'=32,'dp'=4] {'tp'}, use_global_device_ids=true, to_apply=%region_6.7 | all-reduce | flops 1048576 | bytes 6291456 | tf_op jit(solution)/shard_map/psum | solution.py:128
  464.4 64.7 %psum.15 = f32[2048]{0:T(1024)S(1)} all-reduce(f32[2048]{0:T(1024)S(1)} %get-tuple-element.206), channel_id=1, replica_groups=mesh['tp'=2,'sp'=32,'dp'=4] {'sp'}, use_global_device_ids=true, to_apply=%region_8.9 | all-reduce | flops 2048 | bytes 16384 | tf_op jit(solution)/shard_map/psum | solution.py:133
  (120 shorter events, 152.2 us)
Async XLA Ops:
  7.2 11.8 %copy-start.2 = (s32[4096]{0:T(1024)S(1)}, s32[4096]{0:T(1024)}, u32[]{:S(2)}) copy-start(s32[4096]{0:T(1024)} %param.15) | copy-start | bytes 49156
  7.2 12.0 %copy-start.1 = (bf16[128,2048]{1,0:T(8,128)(2,1)S(1)}, bf16[128,2048]{1,0:T(8,128)(2,1)}, u32[]{:S(2)}) copy-start(bf16[128,2048]{1,0:T(8,128)(2,1)} %param.12) | copy-start | bytes 1572868
  7.2 66.2 %all-gather.3.cloned.1.call-start = ((), (), s32[]{:S(2)}) async-start(), calls=%async_computation.2 | async-start | bytes 2162688 | tf_op jit(solution)/shard_map/all_gather | solution.py:81
  10.3 37.9 %all-to-all-start.1 = ((bf16[32,128,256]{2,1,0:T(8,128)(2,1)}), bf16[32,128,256]{2,1,0:T(8,128)(2,1)S(1)}, u32[]{:S(2)}, u32[]{:S(2)}) async-start(bf16[32,128,256]{2,1,0:T(8,128)(2,1)} %tile.2), calls=%async_computation.1 | async-start | bytes 4194304 | tf_op jit(solution)/shard_map/all_to_all | solution.py:20
  48.2 26.5 %all-to-all-start = ((bf16[32,64,128]{2,1,0:T(8,128)(2,1)}), bf16[32,64,128]{2,1,0:T(8,128)(2,1)}, u32[]{:S(2)}, u32[]{:S(2)}) async-start(bf16[32,64,128]{2,1,0:T(8,128)(2,1)} %bitcast.4), calls=%async_computation | async-start | bytes 1048576 | tf_op jit(solution)/shard_map/all_to_all | solution.py:79
  53.2 131.0 %all-gather.5.cloned.1.call-start = ((), (), s32[]{:S(2)}) async-start(), calls=%async_computation.3 | async-start | bytes 17301504 | tf_op jit(solution)/shard_map/all_gather | solution.py:109
  74.7 31.0 %copy-start.4 = (s32[256]{0:T(256)S(1)}, s32[256]{0:T(256)}, u32[]{:S(2)}) copy-start(s32[256]{0:T(256)} %param.19) | copy-start | bytes 3076
  362.5 166.6 %copy-start.3 = (f32[256]{0:T(256)S(1)}, f32[256]{0:T(256)}, u32[]{:S(2)}) copy-start(f32[256]{0:T(256)} %param.18) | copy-start | bytes 3076
  464.4 66.2 %copy-start = (bf16[2048,256]{1,0:T(8,128)(2,1)}, bf16[2048,256]{1,0:T(8,128)(2,1)S(1)}, u32[]{:S(2)}) copy-start(bf16[2048,256]{1,0:T(8,128)(2,1)S(1)} %get-tuple-element.207) | copy-start | bytes 3145732
Sparse Core Ops, SparseCore 0:
  10.5 62.7 all-gather.2
  105.8 78.3 all-gather.4
